TPU v7x, 512 devices: a whole 4x4x16 slice. The times are simulated.
512 devices in a mesh: dp: 16 (over z), tensor: 32 (over x, y, core).
Axes of the slice: x: 4, y: 4, z: 16, core: 2. Of those that a mesh axis runs over, the one named last changes fastest.
Arguments:
- pages: bfloat16 [2, 64, 64, 2048], P(None, 'dp', None, 'tensor'), may hold values from -8 to 8
- page_table: int32 [16, 2], replicated, may hold values from 0 to 63, as said below
- page_count: int32 [16], replicated, may hold values from 1 to 2
- last_len: int32 [16], replicated, may hold values from 1 to 64
- targets: int32 [16, 128], P('dp'), may hold values from 0 to 65535
- mix_key: float32 [2, 2048], P(None, 'tensor'), may hold values from 0.05 to 0.95
- w_key: bfloat16 [2, 2048, 8192], P(None, None, 'tensor'), may hold values from -0.125 to 0.125
- w_value: bfloat16 [2, 8192, 2048], P(None, 'tensor'), may hold values from -0.0625 to 0.0625
- ln_gain: float32 [2, 2048], replicated, may hold values from 0.5 to 1.5
- ln_bias: float32 [2, 2048], replicated, may hold values from -2 to 2
- head: bfloat16 [2, 2048, 65536], P(None, 'dp', 'tensor'), may hold values from -8 to 8
Outputs:
- token_logprob: float32 [16, 128], P('dp', 'tensor')
- ratio_sum: float32 [16], P('dp')
Inputs may be any that keep to these rules, and one draw needn't show every extreme that they name: Entries are distinct; the page lives on dp device page_table[r, p] // 4.
All inputs are finite; a program needn't handle non-finite values.
Results may differ from a plain program's by a relative error of at most 0.0029.
The roundings to bfloat16 on the way count: a program that leaves them out, or rounds other values in their place, can miss the bound.
Values may be sent and summed in bfloat16 or wider, within the bound.
A program may use at most 128 MiB of HBM per device.

v0:
```python
import jax
import jax.numpy as jnp
from jax import lax
from jax.sharding import PartitionSpec as P

D = 2048
epsilon = 1e-05


def joined(value, axis, join):
    pieces = jax.tree.map(lambda part: lax.all_gather(part, axis), value)
    head = jax.tree.map(lambda part: part[0], pieces)
    tail = jax.tree.map(lambda part: part[1:], pieces)
    total, _ = lax.scan(lambda total, piece: (join(total, piece), None), head, tail)
    return total


def combine(left_stats, right_stats):
    peak = jnp.maximum(left_stats[0], right_stats[0])
    totals = left_stats[1] * jnp.exp(left_stats[0] - peak) + right_stats[1] * jnp.exp(
        right_stats[0] - peak
    )
    return (peak, totals, left_stats[2] + right_stats[2])


def body(
    pages,
    page_table,
    page_count,
    last_len,
    targets,
    mix_key,
    w_key,
    w_value,
    ln_gain,
    ln_bias,
    head,
):
    tensor_count = lax.axis_size("tensor")
    owner = lax.axis_index("dp")
    tensor_index = lax.axis_index("tensor")
    page_len = pages.shape[2]
    width_local = pages.shape[3]
    page_cap = page_table.shape[1]
    slot_count = page_cap * page_len
    live_pages = jnp.arange(page_cap)[None, :] < page_count[:, None]
    table_row = page_table[owner]
    everything = lax.all_gather(pages, "dp", axis=1, tiled=True)
    states = jnp.take(everything, table_row, axis=1)
    states = jnp.where(live_pages[owner][None, :, None, None], states, jnp.zeros_like(states))
    states = states.reshape(2, slot_count, width_local)
    state_f = states.astype(jnp.float32)
    previous = jnp.concatenate(
        [jnp.zeros((2, 1, width_local), jnp.float32), state_f[:, :-1]], axis=1
    )
    shifted = (state_f + (previous - state_f) * mix_key[:, None, :]).astype(jnp.bfloat16)
    hidden = jnp.einsum(
        "msd,mdf->msf",
        lax.all_gather(shifted, "tensor", axis=2, tiled=True),
        w_key,
        preferred_element_type=jnp.float32,
    )
    key_act = (jnp.maximum(hidden, 0.0) ** 2).astype(jnp.bfloat16)
    partial_out = jnp.einsum("msf,mfd->msd", key_act, w_value, preferred_element_type=jnp.float32)
    ffn_out = lax.psum_scatter(partial_out, "tensor", scatter_dimension=2, tiled=True)
    residual = state_f + ffn_out
    row_sum, row_square = lax.psum(
        (jnp.sum(residual, axis=-1), jnp.sum(residual * residual, axis=-1)), "tensor"
    )
    average = row_sum / D
    variance = row_square / D - average * average
    gain_local = lax.dynamic_slice_in_dim(ln_gain, tensor_index * width_local, width_local, 1)
    bias_local = lax.dynamic_slice_in_dim(ln_bias, tensor_index * width_local, width_local, 1)
    normed_local = (
        (residual - average[..., None])
        * lax.rsqrt(variance + epsilon)[..., None]
        * gain_local[:, None, :]
        + bias_local[:, None, :]
    ).astype(jnp.bfloat16)
    normed = lax.all_gather(normed_local, "tensor", axis=2, tiled=True)
    vocab_local = head.shape[2]
    logits = jnp.einsum(
        "msd,mdv->msv",
        normed,
        lax.all_gather(head, "dp", axis=1, tiled=True),
        preferred_element_type=jnp.float32,
    )
    peak = jnp.max(logits, axis=-1)
    totals = jnp.sum(jnp.exp(logits - peak[..., None]), axis=-1)
    vocab_ids = jnp.arange(vocab_local) + tensor_index * vocab_local
    matches = vocab_ids[None, None, :] == targets[0][None, :, None]
    target_logit = jnp.sum(jnp.where(matches, logits, 0.0), axis=-1)
    peak, totals, target_logit = joined((peak, totals, target_logit), "tensor", combine)
    logp = target_logit - peak - jnp.log(totals)
    length = (page_count[owner] - 1) * page_len + last_len[owner]
    valid = jnp.arange(slot_count) < length
    policy_row = jnp.where(valid, logp[0], 0.0)
    ratio = jnp.sum(jnp.where(valid, logp[0] - logp[1], 0.0))
    share = slot_count // tensor_count
    token_part = lax.dynamic_slice_in_dim(policy_row, tensor_index * share, share)[None, :]
    return (token_part, ratio[None])


def solution(mesh):
    placed = (
        P(None, "dp", None, "tensor"),
        P(),
        P(),
        P(),
        P("dp", None),
        P(None, "tensor"),
        P(None, None, "tensor"),
        P(None, "tensor", None),
        P(),
        P(),
        P(None, "dp", "tensor"),
    )
    return jax.shard_map(
        body, mesh=mesh, in_specs=placed, out_specs=(P("dp", "tensor"), P("dp")), check_vma=False
    )
```

profile of v0, /device:TPU:1, one launch (start us, length us, event | category | flops | bytes accessed | tf_op | source)
XLA Modules:
  0.0 654.3 jit_solution(647617080670465465)
XLA Ops:
  7.2 0.7 all-gather.11.cloned.1.call-update
  8.0 0.9 dynamic-slice_reduce_fusion
  8.8 1.2 dynamic_slice.31
  10.1 0.7 compare_bitcast_fusion
  10.8 0.1 broadcast_in_dim.66
  10.9 0.1 broadcast_in_dim.68
  11.0 0.1 broadcast_in_dim.69
  11.1 68.5 %all-gather.11.cloned.1.call-done = bf16[2,64,64,64]{3,2,1,0:T(8,128)(2,1)} async-done(((bf16[2,4,64,64]{3,2,1,0:T(8,128)(2,1)}), bf16[2,64,64,64]{3,2,1,0:T(8,128)(2,1)}) %all-gather.11.cloned.1.call-update) | async-done | bytes 1048592 | tf_op jit(solution)/shard_map/all_gather | solution.py:48
  79.6 2.2 gather_fusion
  81.7 0.1 copy.15
  81.8 0.1 gather.7
  81.9 1.4 add_convert_fusion.1
  83.4 64.8 %all-gather.13.cloned.1.call-done = bf16[2,128,2048]{1,2,0:T(8,128)(2,1)} async-done(((bf16[2,128,64]{1,2,0:T(8,128)(2,1)}), bf16[2,128,2048]{1,2,0:T(8,128)(2,1)}) %all-gather.13.cloned.1.call-update) | async-done | bytes 1048592 | tf_op jit(solution)/shard_map/all_gather | solution.py:59
  148.2 4.5 fusion.4
  152.8 0.8 constant_dynamic-slice_fusion.1
  153.6 98.6 %reduce-scatter.2.cloned.1.call-done = f32[2,128,64]{1,2,0:T(8,128)} async-done(((f32[2,128,2048]{1,2,0:T(8,128)}), f32[2,128,64]{1,2,0:T(8,128)}) %reduce-scatter.2.cloned.1.call-update) | async-done | bytes 65552 | tf_op jit(solution)/shard_map/reduce_scatter | solution.py:65
  252.1 0.9 fusion.6
  253.0 64.3 %all-reduce.1 = (f32[2,128]{1,0:T(2,128)S(1)}, f32[2,128]{1,0:T(2,128)S(1)}) all-reduce(f32[2,128]{1,0:T(2,128)S(1)} %get-tuple-element.47, f32[2,128]{1,0:T(2,128)S(1)} %get-tuple-element.46), channel_id=1, replica_groups=mesh['dp'=16,'tensor'=32] {'tensor'}, use_global_device_ids=true, to_apply=%region_4.5 | all-reduce | flops 512 | bytes 4096 | tf_op jit(solution)/shard_map/psum | solution.py:67
  317.3 1.6 add_convert_fusion
  319.0 0.5 all-gather.17.cloned.1.call-update
  320.2 0.6 dynamic_slice.32
  321.4 0.2 broadcast_compare_fusion
  321.7 53.0 %all-gather.15.cloned.1.call-done = bf16[2,128,2048]{1,2,0:T(8,128)(2,1)} async-done(((bf16[2,128,64]{1,2,0:T(8,128)(2,1)}), bf16[2,128,2048]{1,2,0:T(8,128)(2,1)}) %all-gather.15.cloned.1.call-update) | async-done | bytes 1048592 | tf_op jit(solution)/shard_map/all_gather | solution.py:80
  374.6 191.1 %all-gather.17.cloned.1.call-done = bf16[2,2048,2048]{2,1,0:T(8,128)(2,1)} async-done(((bf16[2,128,2048]{2,1,0:T(8,128)(2,1)}), bf16[2,2048,2048]{2,1,0:T(8,128)(2,1)}) %all-gather.17.cloned.1.call-update) | async-done | bytes 16777232 | tf_op jit(solution)/shard_map/all_gather | solution.py:85
  565.7 8.6 %fusion.11 = (f32[2,128]{1,0:T(2,128)S(1)}, f32[2,128,2048]{2,1,0:T(8,128)S(1)}) fusion(bf16[2,128,2048]{1,2,0:T(8,128)(2,1)} %all-gather.15.cloned.1.call-done, bf16[2,2048,2048]{2,1,0:T(8,128)(2,1)} %all-gather.17.cloned.1.call-done), kind=kOutput, calls=%fused_computation.45 | convolution fusion | flops 2148007680 | bytes 19923968 | tf_op jit(solution)/shard_map/msd,mdv->msv/dot_general | solution.py:82
  574.4 0.7 select_reduce_fusion
  575.1 24.7 %all-gather.5 = f32[32,2,128]{2,1,0:T(2,128)S(1)} all-gather(f32[1,2,128]{2,1,0:T(2,128)S(1)} %bitcast.56), channel_id=4, replica_groups=mesh['dp'=16,'tensor'=32] {'tensor'}, dimensions={0}, use_global_device_ids=true | all-gather | bytes 33792 | tf_op jit(solution)/shard_map/all_gather | solution.py:11
  599.8 23.5 %all-gather.4 = f32[32,2,128]{2,1,0:T(2,128)S(1)} all-gather(f32[1,2,128]{2,1,0:T(2,128)S(1)} %bitcast.55), channel_id=3, replica_groups=mesh['dp'=16,'tensor'=32] {'tensor'}, dimensions={0}, use_global_device_ids=true | all-gather | bytes 33792 | tf_op jit(solution)/shard_map/all_gather | solution.py:11
  623.3 21.9 %all-gather.3 = f32[32,2,128]{2,1,0:T(2,128)S(1)} all-gather(f32[1,2,128]{2,1,0:T(2,128)S(1)} %bitcast.54), channel_id=2, replica_groups=mesh['dp'=16,'tensor'=32] {'tensor'}, dimensions={0}, use_global_device_ids=true | all-gather | bytes 33792 | tf_op jit(solution)/shard_map/all_gather | solution.py:11
  645.2 1.3 while.14
  646.5 0.6 fusion.7
  647.1 0.6 dynamic-slice_bitcast_fusion
  (59 shorter events, 1.3 us)
Async XLA Ops:
  7.2 141.0 %copy-start = (bf16[2,256,2048]{2,1,0:T(8,128)(2,1)S(1)}, bf16[2,256,2048]{2,1,0:T(8,128)(2,1)}, u32[]{:S(2)}) copy-start(bf16[2,256,2048]{2,1,0:T(8,128)(2,1)} %param.20) | copy-start | bytes 6291460
  7.2 72.4 %all-gather.11.cloned.1.call-start = ((), (), s32[]{:S(2)}) async-start(), calls=%async_computation.1 | async-start | bytes 2228224 | tf_op jit(solution)/shard_map/all_gather | solution.py:48
  7.9 140.3 %all-gather.13.cloned.1.call-start = ((), (), s32[]{:S(2)}) async-start(), calls=%async_computation.2 | async-start | bytes 1081344 | tf_op jit(solution)/shard_map/all_gather | solution.py:59
  83.4 168.8 %reduce-scatter.2.cloned.1.call-start = ((), (), s32[]{:S(2)}) async-start(), calls=%async_computation.3 | async-start | bytes 2162688 | tf_op jit(solution)/shard_map/reduce_scatter | solution.py:65
  152.7 167.5 %copy-start.2 = (s32[16]{0:T(128)S(1)}, s32[16]{0:T(128)}, u32[]{:S(2)}) copy-start(s32[16]{0:T(128)} %param.16) | copy-start | bytes 196
  152.7 168.7 %copy-start.1 = (s32[1,128]{1,0:T(1,128)S(1)}, s32[1,128]{1,0:T(1,128)}, u32[]{:S(2)}) copy-start(s32[1,128]{1,0:T(1,128)} %param.17) | copy-start | bytes 1540
  152.7 221.9 %all-gather.15.cloned.1.call-start = ((), (), s32[]{:S(2)}) async-start(), calls=%async_computation.4 | async-start | bytes 1081344 | tf_op jit(solution)/shard_map/all_gather | solution.py:80
  318.9 246.8 %all-gather.17.cloned.1.call-start = ((), (), s32[]{:S(2)}) async-start(), calls=%async_computation.5 | async-start | bytes 17825792 | tf_op jit(solution)/shard_map/all_gather | solution.py:85
Sparse Core Ops, SparseCore 0:
  10.1 69.4 all-gather.10
  83.5 64.6 all-gather.12
  152.9 99.2 reduce-scatter.1
  319.0 55.5 all-gather.14
  376.5 189.1 all-gather.16
where the time goes:
time: 655 us; the launch traced here: 654 us
  waiting for transfers between devices  477 us (73%)
  blocking collectives  134 us (20%)
  between operations  15.2 us (2%)
  matrix products  13.2 us (2%)
  other arithmetic  6.97 us (1%)
  local copies, waits for them, and re-layouts  6.76 us (1%)
    all_gather x1, waiting for transfers between devices, body(): lax.all_gather(head, 'dp', axis=1, tiled=True)  191 us
    reduce_scatter x1, waiting for transfers between devices, body(): lax.psum_scatter(partial_out, 'tensor', scatter_dimension=2, tiled=True)  98.6 us
    all_gather x3, blocking collectives, joined(): pieces = jax.tree.map(lambda part: lax.all_gather(part, axis), value)  70.1 us
    all_gather x1, waiting for transfers between devices, body(): everything = lax.all_gather(pages, 'dp', axis=1, tiled=True)  68.5 us
    all_gather x1, waiting for transfers between devices, body(): lax.all_gather(shifted, 'tensor', axis=2, tiled=True)  64.8 us
    psum x1, blocking collectives, body(): lax.psum((jnp.sum(residual, axis=-1), jnp.sum(residual * residual, axis=-...  64.3 us
    all_gather x1, waiting for transfers between devices, body(): normed = lax.all_gather(normed_local, 'tensor', axis=2, tiled=True)  53 us
  transfers between devices with their start and end apart: 5, of which 5 were waited for; matrix products, arithmetic and copies ran while one was open for 1% of the time, Pallas kernels for 0%

commit v1 on v0

--- a/solution.py
+++ b/solution.py
@@ -82,7 +82,9 @@
     logits = jnp.einsum(
         "msd,mdv->msv",
         normed,
-        lax.all_gather(head, "dp", axis=1, tiled=True),
+        jnp.concatenate(
+            lax.all_to_all(jnp.stack([head] * lax.axis_size("dp")), "dp", 0, 0), axis=1
+        ),
         preferred_element_type=jnp.float32,
     )
     peak = jnp.max(logits, axis=-1)

time: 655 us -> 877 us (1.34)
  waiting for transfers between devices: 477 us -> 661 us
  local copies, waits for them, and re-layouts: 6.76 us -> 26.6 us
  starting transfers between devices: 0.2 us -> 16.1 us
    all_to_all x0 -> x1, waiting for transfers between devices: none -> 309 us  [body(): lax.all_to_all(jnp.stack([head] * lax.axis_size('dp')), 'dp', 0, 0)]
    all_gather x1 -> x0, waiting for transfers between devices: 191 us -> none  [body(): lax.all_gather(head, 'dp', axis=1, tiled=True)]
    all_gather x1, waiting for transfers between devices: 68.5 us -> 185 us  [body(): everything = lax.all_gather(pages, 'dp', axis=1, tiled=True)]
    all_gather x1, waiting for transfers between devices: 53 us -> 0.01 us  [body(): normed = lax.all_gather(normed_local, 'tensor', axis=2, tiled=True)]
    all_to_all x0 -> x1, starting transfers between devices: none -> 15.9 us  [body(): lax.all_to_all(jnp.stack([head] * lax.axis_size('dp')), 'dp', 0, 0)]
    reshape x0 -> x1, local copies, waits for them, and re-layouts: none -> 14.1 us  [body(): jnp.concatenate(lax.all_to_all(jnp.stack([head] * lax.axis_size('dp')), '...]
  transfers between devices with their start and end apart: 5 -> 5, of which waited for: 5 -> 4; matrix products, arithmetic and copies ran while one was open for 1% -> 3% of each run, Pallas kernels for 0% -> 0%
where the time goes in v1:
time: 877 us; the launch traced here: 876 us
  waiting for transfers between devices  661 us (75%)
  blocking collectives  137 us (16%)
  local copies, waits for them, and re-layouts  26.6 us (3%)
  starting transfers between devices  16.1 us (2%)
  between operations  15.2 us (2%)
  matrix products  13.1 us (1%)
    all_to_all x1, waiting for transfers between devices, body(): lax.all_to_all(jnp.stack([head] * lax.axis_size('dp')), 'dp', 0, 0)  309 us
    all_gather x1, waiting for transfers between devices, body(): everything = lax.all_gather(pages, 'dp', axis=1, tiled=True)  185 us
    reduce_scatter x1, waiting for transfers between devices, body(): lax.psum_scatter(partial_out, 'tensor', scatter_dimension=2, tiled=True)  98.9 us
    all_gather x3, blocking collectives, joined(): pieces = jax.tree.map(lambda part: lax.all_gather(part, axis), value)  71.1 us
    all_gather x1, waiting for transfers between devices, body(): lax.all_gather(shifted, 'tensor', axis=2, tiled=True)  66.9 us
    psum x1, blocking collectives, body(): lax.psum((jnp.sum(residual, axis=-1), jnp.sum(residual * residual, axis=-...  66.3 us
  transfers between devices with their start and end apart: 5, of which 4 were waited for; matrix products, arithmetic and copies ran while one was open for 3% of the time, Pallas kernels for 0%

profile of v1, /device:TPU:1, one launch (start us, length us, event | category | flops | bytes accessed | tf_op | source)
XLA Modules:
  0.0 876.0 jit_solution(6027697861867278011)
XLA Ops:
  7.2 7.0 stack.2
  14.2 15.9 %all-to-all-start = ((bf16[16,2,128,2048]{3,2,1,0:T(8,128)(2,1)}), bf16[16,2,128,2048]{3,2,1,0:T(8,128)(2,1)}, u32[]{:S(2)}, u32[]{:S(2)}) async-start(bf16[16,2,128,2048]{3,2,1,0:T(8,128)(2,1)} %stack.2), calls=%async_computation.1 | async-start | bytes 33554432 | tf_op jit(solution)/shard_map/all_to_all | solution.py:86
  30.2 0.7 all-gather.10.cloned.1.call-update
  31.0 0.2 dynamic-slice_reduce_fusion
  31.1 0.6 dynamic_slice.31
  31.7 0.7 compare_bitcast_fusion
  32.5 0.1 broadcast_in_dim.66
  32.6 0.1 broadcast_in_dim.69
  32.7 184.9 %all-gather.10.cloned.1.call-done = bf16[2,64,64,64]{3,2,1,0:T(8,128)(2,1)} async-done(((bf16[2,4,64,64]{3,2,1,0:T(8,128)(2,1)}), bf16[2,64,64,64]{3,2,1,0:T(8,128)(2,1)}) %all-gather.10.cloned.1.call-update) | async-done | bytes 1048592 | tf_op jit(solution)/shard_map/all_gather | solution.py:48
  217.7 2.2 gather_fusion
  219.8 0.1 copy.15
  219.9 0.1 gather.7
  220.1 0.7 add_convert_fusion.1
  220.9 66.9 %all-gather.12.cloned.1.call-done = bf16[2,128,2048]{1,2,0:T(8,128)(2,1)} async-done(((bf16[2,128,64]{1,2,0:T(8,128)(2,1)}), bf16[2,128,2048]{1,2,0:T(8,128)(2,1)}) %all-gather.12.cloned.1.call-update) | async-done | bytes 1048592 | tf_op jit(solution)/shard_map/all_gather | solution.py:59
  287.7 4.5 fusion.4
  292.3 0.8 constant_dynamic-slice_fusion.1
  293.1 98.9 %reduce-scatter.2.cloned.1.call-done = f32[2,128,64]{1,2,0:T(8,128)} async-done(((f32[2,128,2048]{1,2,0:T(8,128)}), f32[2,128,64]{1,2,0:T(8,128)}) %reduce-scatter.2.cloned.1.call-update) | async-done | bytes 65552 | tf_op jit(solution)/shard_map/reduce_scatter | solution.py:65
  392.0 0.9 fusion.6
  392.9 66.3 %all-reduce.1 = (f32[2,128]{1,0:T(2,128)S(1)}, f32[2,128]{1,0:T(2,128)S(1)}) all-reduce(f32[2,128]{1,0:T(2,128)S(1)} %get-tuple-element.47, f32[2,128]{1,0:T(2,128)S(1)} %get-tuple-element.46), channel_id=1, replica_groups=mesh['dp'=16,'tensor'=32] {'tensor'}, use_global_device_ids=true, to_apply=%region_4.5 | all-reduce | flops 512 | bytes 4096 | tf_op jit(solution)/shard_map/psum | solution.py:67
  459.2 1.6 add_convert_fusion
  461.4 0.6 dynamic_slice.32
  462.7 0.2 broadcast_compare_fusion
  462.9 309.4 %all-to-all-done = bf16[16,2,128,2048]{3,2,1,0:T(8,128)(2,1)} async-done(((bf16[16,2,128,2048]{3,2,1,0:T(8,128)(2,1)}), bf16[16,2,128,2048]{3,2,1,0:T(8,128)(2,1)}, u32[]{:S(2)}, u32[]{:S(2)}) %all-to-all-start) | async-done | bytes 16777248 | tf_op jit(solution)/shard_map/all_to_all | solution.py:86
  772.3 14.1 %copy.17 = bf16[2,16,128,2048]{3,2,1,0:T(8,128)(2,1)} copy(bf16[2,16,128,2048]{3,2,0,1:T(8,128)(2,1)} %bitcast.7) | data formatting | bytes 33554432 | tf_op jit(solution)/shard_map/reshape | solution.py:85
  786.4 8.6 fusion.11
  795.1 0.7 select_reduce_fusion
  795.8 25.7 %all-gather.5 = f32[32,2,128]{2,1,0:T(2,128)S(1)} all-gather(f32[1,2,128]{2,1,0:T(2,128)S(1)} %bitcast.59), channel_id=4, replica_groups=mesh['dp'=16,'tensor'=32] {'tensor'}, dimensions={0}, use_global_device_ids=true | all-gather | bytes 33792 | tf_op jit(solution)/shard_map/all_gather | solution.py:11
  821.5 23.5 %all-gather.4 = f32[32,2,128]{2,1,0:T(2,128)S(1)} all-gather(f32[1,2,128]{2,1,0:T(2,128)S(1)} %bitcast.58), channel_id=3, replica_groups=mesh['dp'=16,'tensor'=32] {'tensor'}, dimensions={0}, use_global_device_ids=true | all-gather | bytes 33792 | tf_op jit(solution)/shard_map/all_gather | solution.py:11
  845.0 21.9 %all-gather.3 = f32[32,2,128]{2,1,0:T(2,128)S(1)} all-gather(f32[1,2,128]{2,1,0:T(2,128)S(1)} %bitcast.57), channel_id=2, replica_groups=mesh['dp'=16,'tensor'=32] {'tensor'}, dimensions={0}, use_global_device_ids=true | all-gather | bytes 33792 | tf_op jit(solution)/shard_map/all_gather | solution.py:11
  866.9 1.3 while.14
  868.3 0.6 fusion.7
  868.9 0.6 dynamic-slice_bitcast_fusion
  (66 shorter events, 1.3 us)
Async XLA Ops:
  7.2 280.6 %copy-start = (bf16[2,256,2048]{2,1,0:T(8,128)(2,1)S(1)}, bf16[2,256,2048]{2,1,0:T(8,128)(2,1)}, u32[]{:S(2)}) copy-start(bf16[2,256,2048]{2,1,0:T(8,128)(2,1)} %param.20) | copy-start | bytes 6291460
  14.2 16.7 %copy-start.2 = (s32[16,2]{0,1:T(2,128)S(1)}, s32[16,2]{0,1:T(2,128)}, u32[]{:S(2)}) copy-start(s32[16,2]{0,1:T(2,128)} %param.14) | copy-start | bytes 388
  14.2 16.9 %copy-start.4 = (s32[16]{0:T(128)S(1)}, s32[16]{0:T(128)}, u32[]{:S(2)}) copy-start(s32[16]{0:T(128)} %param.15) | copy-start | bytes 196
  14.2 205.9 %copy-start.1 = (f32[2,64]{1,0:T(2,128)S(1)}, f32[2,64]{1,0:T(2,128)}, u32[]{:S(2)}) copy-start(f32[2,64]{1,0:T(2,128)} %param.18) | copy-start | bytes 1540
  14.2 758.1 %all-to-all-start = ((bf16[16,2,128,2048]{3,2,1,0:T(8,128)(2,1)}), bf16[16,2,128,2048]{3,2,1,0:T(8,128)(2,1)}, u32[]{:S(2)}, u32[]{:S(2)}) async-start(bf16[16,2,128,2048]{3,2,1,0:T(8,128)(2,1)} %stack.2), calls=%async_computation.1 | async-start | bytes 33554432 | tf_op jit(solution)/shard_map/all_to_all | solution.py:86
  30.2 187.5 %all-gather.10.cloned.1.call-start = ((), (), s32[]{:S(2)}) async-start(), calls=%async_computation.2 | async-start | bytes 2228224 | tf_op jit(solution)/shard_map/all_gather | solution.py:48
  30.9 256.8 %all-gather.12.cloned.1.call-start = ((), (), s32[]{:S(2)}) async-start(), calls=%async_computation.3 | async-start | bytes 1081344 | tf_op jit(solution)/shard_map/all_gather | solution.py:59
  220.8 171.2 %reduce-scatter.2.cloned.1.call-start = ((), (), s32[]{:S(2)}) async-start(), calls=%async_computation.4 | async-start | bytes 2162688 | tf_op jit(solution)/shard_map/reduce_scatter | solution.py:65
  292.2 169.2 %copy-start.5 = (s32[16]{0:T(128)S(1)}, s32[16]{0:T(128)}, u32[]{:S(2)}) copy-start(s32[16]{0:T(128)} %param.16) | copy-start | bytes 196
  292.2 170.4 %copy-start.3 = (s32[1,128]{1,0:T(1,128)S(1)}, s32[1,128]{1,0:T(1,128)}, u32[]{:S(2)}) copy-start(s32[1,128]{1,0:T(1,128)} %param.17) | copy-start | bytes 1540
  292.3 494.2 %all-gather.14.cloned.1.call-start = ((), (), s32[]{:S(2)}) async-start(), calls=%async_computation.5 | async-start | bytes 1081344 | tf_op jit(solution)/shard_map/all_gather | solution.py:80
Sparse Core Ops, SparseCore 0:
  33.1 184.5 all-gather.9
  220.9 66.7 all-gather.11
  292.4 99.5 reduce-scatter.1
  460.9 56.2 all-gather.13
